TPU v7x, 512 devices: a whole 4x8x8 slice. The times are simulated.
512 devices in a mesh: dp: 2 (over core), ctx: 32 (over x, y), tp: 8 (over z).
Axes of the slice: x: 4, y: 8, z: 8, core: 2. Of those that a mesh axis runs over, the one named last changes fastest.
Arguments:
- x_in: bfloat16 [2, 16384, 8192], P('dp', 'ctx', 'tp'), may hold values from -6 to 6
- grad_out: bfloat16 [2, 16384, 8192], P('dp', 'ctx', 'tp'), may hold values from -16 to 16
- state_maps: bfloat16 [2, 16384, 256], P('dp', 'ctx'), may hold values from -0.875 to 0.875
- dt_raw: float32 [2, 128, 16384], P('dp', 'tp', 'ctx'), may hold values from -3 to 20
- a_log: float32 [128], P('tp'), may hold values from -12 to 0
- saved_states: float32 [2, 32, 128, 64, 128], P('dp', 'ctx', 'tp'), may hold values from -0.625 to 0.625
- layer_in: bfloat16 [2, 16384, 8192], P('dp', 'ctx', 'tp'), may hold values from -40 to 40
- doc_lengths: int32 [2, 4], P('dp'), may hold values from 1 to 8192, 16384 in all within a row
Outputs:
- grad_x: bfloat16 [2, 16384, 8192], P('dp', 'ctx', 'tp')
- grad_maps: float32 [2, 16384, 256], P('dp', ('ctx', 'tp'))
- grad_dt_proj: float32 [128, 8192], P(('dp', 'ctx'), 'tp')
All inputs are finite; a program needn't handle non-finite values.
Results may differ from a plain program's by a relative error of at most 0.0055.
Values may be sent and summed in bfloat16 or wider, within the bound.
No kernel may reach another device: no remote copies, remote signals or barrier semaphores. Data moves between devices by JAX's collectives and lax.ppermute only.
A program may use at most 128 MiB of HBM per device.

v0:
```python
import jax
import jax.numpy as jnp
from jax import lax
from jax.sharding import Mesh
from jax.sharding import PartitionSpec as P

HEAD_DIM = 64
STATE = 128
CTX = ("ctx_0", "ctx_1")
DP_CTX = ("dp", "ctx_0", "ctx_1")
CTX_TP = ("ctx_0", "ctx_1", "tp")


head_group = 4
epsilon = 1e-06


def neutral_like(x, identity):
    return jax.tree.map(
        lambda a, e: jnp.broadcast_to(jnp.asarray(e, a.dtype), a.shape), x, identity
    )


def carried_in(x, axes, combine, identity):
    before = start = neutral_like(x, identity)
    subtotal = x
    for axis in reversed(axes):
        count, position = (lax.axis_size(axis), lax.axis_index(axis))
        pieces = jax.tree.map(lambda part: lax.all_gather(part, axis), subtotal)
        inside, subtotal = (start, start)
        for k in reversed(range(count)):
            passed = k > position
            subtotal = combine(subtotal, jax.tree.map(lambda part: part[k], pieces))
            inside = jax.tree.map(lambda new, old: jnp.where(passed, new, old), subtotal, inside)
        before = combine(inside, before)
    return before


def laid_out(blocks, dim):
    blocks = jnp.moveaxis(blocks, 0, dim)
    dims = blocks.shape
    return blocks.reshape(*dims[:dim], dims[dim] * dims[dim + 1], *dims[dim + 2 :])


def sent_to_all(x, axis):
    copies = jnp.broadcast_to(x, (lax.axis_size(axis), *x.shape))
    return lax.all_to_all(copies, axis, split_axis=0, concat_axis=0, tiled=True)


def gather_directly(x, axis, dim):
    return laid_out(sent_to_all(x, axis), dim)


def in_blocks(x, dim, count):
    dims = x.shape
    blocks = x.reshape(*dims[:dim], count, dims[dim] // count, *dims[dim + 1 :])
    return jnp.moveaxis(blocks, dim, 0)


def summed_on_arrival(x, axis, dim):
    count = lax.axis_size(axis)
    blocks = lax.all_to_all(in_blocks(x, dim, count), axis, 0, 0, tiled=True)
    return jnp.sum(blocks, axis=0)


def of_everyone(x, axis):
    everything = sent_to_all(x, axis)
    return jnp.sum(everything, axis=0)


def segments(lengths_row, anchor, length):
    doc_ends = jnp.cumsum(lengths_row)
    positions = anchor + jnp.arange(length, dtype=jnp.int32)
    labels = jnp.sum((positions[:, None] >= doc_ends[None, :]).astype(jnp.int32), axis=1)
    before = jnp.sum((anchor - 1 >= doc_ends).astype(jnp.int32))
    before = jnp.where(anchor > 0, before, -1)
    return (labels, before)


def quad_terms(cumulative, step_sizes_delta, x_rows, dy_rows, pair_dot, causal):
    length, head_count, head_width = x_rows.shape

    def one_group(group_index, running):
        mixed_sum, r_local, dc_local = running
        offset = group_index * head_group
        c_part = lax.dynamic_slice_in_dim(cumulative, offset, head_group, 0)
        d_part = lax.dynamic_slice_in_dim(step_sizes_delta, offset, head_group, 0)
        x_part = lax.dynamic_slice_in_dim(x_rows, offset, head_group, 1)
        y_part = lax.dynamic_slice_in_dim(dy_rows, offset, head_group, 1)
        log_diffs = c_part[:, :, None] - c_part[:, None, :]
        kernel = jnp.where(causal[None], jnp.exp(jnp.where(causal[None], log_diffs, 0.0)), 0.0)
        weighted = kernel * pair_dot[None]
        rounded = weighted.astype(jnp.bfloat16)
        inner_dt = (
            jnp.einsum("ihp,jhp->hij", y_part, x_part, preferred_element_type=jnp.float32)
            * d_part[:, None, :]
        )
        r_part = jnp.einsum("hij,ihp->jhp", rounded, y_part, preferred_element_type=jnp.float32)
        products = weighted * inner_dt
        dc_part = jnp.sum(products, axis=2) - jnp.sum(products, axis=1)
        mixed_sum = mixed_sum + jnp.sum(kernel * inner_dt, axis=0)
        r_local = lax.dynamic_update_slice_in_dim(r_local, r_part, offset, 1)
        dc_local = lax.dynamic_update_slice_in_dim(dc_local, dc_part, offset, 0)
        return (mixed_sum, r_local, dc_local)

    initial = (
        jnp.zeros((length, length), jnp.float32),
        jnp.zeros((length, head_count, head_width), jnp.float32),
        jnp.zeros((head_count, length), jnp.float32),
    )
    return lax.fori_loop(0, head_count // head_group, one_group, initial)


def combine(earlier, later):
    return (earlier[0] * later[0], later[1] + later[0][:, None, None] * earlier[1])


def shards(x_in, grad_out, state_maps, dt_raw, a_log, saved_states, layer_in, doc_lengths):
    high = lax.Precision.HIGHEST
    length = x_in.shape[1]
    head_count = a_log.shape[0]
    x_rows = x_in[0].reshape(length, head_count, HEAD_DIM)
    dy_rows = grad_out[0].reshape(length, head_count, HEAD_DIM)
    b_half = state_maps[0, :, :STATE]
    c_half = state_maps[0, :, STATE:]
    raw_steps = dt_raw[0]
    states = saved_states[0, 0]
    anchor = lax.axis_index(CTX) * length
    labels, before = segments(doc_lengths[0], anchor, length)
    step_sizes_delta = jax.nn.softplus(raw_steps)
    decay_rate = -jnp.exp(a_log)
    cumulative = jnp.cumsum(decay_rate[:, None] * step_sizes_delta, axis=1)
    enter_w = jnp.exp(cumulative) * (labels == before).astype(jnp.float32)[None, :]
    leave_w = (
        jnp.exp(cumulative[:, -1:] - cumulative)
        * (labels == labels[-1]).astype(jnp.float32)[None, :]
    )
    scaled = (jnp.transpose(enter_w)[:, :, None] * dy_rows.astype(jnp.float32)).astype(jnp.bfloat16)
    local_grad = jnp.einsum("ihp,in->hpn", scaled, c_half, preferred_element_type=jnp.float32)
    decay_end = enter_w[:, -1]
    carried_all = carried_in(
        (decay_end, local_grad),
        CTX,
        combine,
        (jnp.ones_like(decay_end), jnp.zeros_like(local_grad)),
    )
    carried = carried_all[1]
    positions = jnp.arange(length)
    causal = (positions[:, None] >= positions[None, :]) & (labels[:, None] == labels[None, :])
    pair_dot = jnp.dot(c_half, b_half.T, preferred_element_type=jnp.float32)
    mixed_sum, r_local, dc_local = quad_terms(
        cumulative, step_sizes_delta, x_rows, dy_rows, pair_dot, causal
    )
    state_term = jnp.einsum(
        "ihp,hpn->in", scaled, states, precision=high, preferred_element_type=jnp.float32
    )
    local_b = jnp.einsum(
        "ij,in->jn", mixed_sum, c_half, precision=high, preferred_element_type=jnp.float32
    )
    local_c = (
        jnp.einsum(
            "ij,jn->in", mixed_sum, b_half, precision=high, preferred_element_type=jnp.float32
        )
        + state_term
    )
    state_c = jnp.einsum(
        "in,hpn->ihp", c_half, states, precision=high, preferred_element_type=jnp.float32
    )
    enter_out = enter_w * jnp.einsum(
        "ihp,ihp->hi", dy_rows, state_c, precision=high, preferred_element_type=jnp.float32
    )
    carry_b = jnp.einsum(
        "jn,hpn->jhp", b_half, carried, precision=high, preferred_element_type=jnp.float32
    )
    carry_r = jnp.transpose(leave_w)[:, :, None] * carry_b
    r_all = r_local + carry_r
    weighted_x = jnp.transpose(step_sizes_delta * leave_w)[:, :, None] * x_rows
    carry_bgrad = jnp.einsum(
        "jhp,hpn->jn", weighted_x, carried, precision=high, preferred_element_type=jnp.float32
    )
    grad_x = (jnp.transpose(step_sizes_delta)[:, :, None] * r_all).astype(jnp.bfloat16)
    w_term = step_sizes_delta * jnp.einsum(
        "jhp,jhp->hj", x_rows, carry_r, precision=high, preferred_element_type=jnp.float32
    )
    v_term = enter_w[:, -1] * jnp.sum(carried * states, axis=(1, 2))
    last_mask = (positions == length - 1).astype(jnp.float32)
    cum_grad = (
        dc_local
        + enter_out
        - w_term
        + (v_term + jnp.sum(w_term, axis=1))[:, None] * last_mask[None, :]
    )
    tail_sum = jnp.flip(jnp.cumsum(jnp.flip(cum_grad, 1), axis=1), 1)
    step_grad = (
        jnp.einsum("jhp,jhp->hj", x_rows, r_all, precision=high, preferred_element_type=jnp.float32)
        + decay_rate[:, None] * tail_sum
    )
    dt_grad = (step_grad * jax.nn.sigmoid(raw_steps)).astype(jnp.bfloat16)
    grad_maps = lax.psum_scatter(
        jnp.concatenate([local_b + carry_bgrad, local_c], axis=1),
        "tp",
        scatter_dimension=0,
        tiled=True,
    )
    gathered = gather_directly(dt_grad, "tp", 0)
    tokens_in = layer_in[0]
    summed = summed_on_arrival(
        jnp.dot(gathered, tokens_in, preferred_element_type=jnp.float32), DP_CTX, 0
    )
    squares = jnp.sum(summed * summed, axis=1)
    own_norm = jnp.sqrt(of_everyone(squares, "tp") + epsilon)
    target = of_everyone(jnp.sum(own_norm), DP_CTX) / gathered.shape[0]
    clip_scale = jnp.minimum(1.0, target / own_norm)
    grad_dt_proj = summed * clip_scale[:, None]
    return (grad_x.reshape(1, length, head_count * HEAD_DIM), grad_maps[None], grad_dt_proj)


def solution(mesh):
    split = Mesh(
        mesh.devices.reshape(mesh.shape["dp"], 4, 8, mesh.shape["tp"]),
        ("dp", "ctx_0", "ctx_1", "tp"),
    )
    return jax.shard_map(
        shards,
        mesh=split,
        in_specs=(
            P("dp", CTX, "tp"),
            P("dp", CTX, "tp"),
            P("dp", CTX, None),
            P("dp", "tp", CTX),
            P("tp"),
            P("dp", CTX, "tp", None, None),
            P("dp", CTX, "tp"),
            P("dp", None),
        ),
        out_specs=(P("dp", CTX, "tp"), P("dp", CTX_TP, None), P(DP_CTX, "tp")),
        check_vma=False,
    )
```

profile of v0, /device:TPU:1, one launch (start us, length us, event | category | flops | bytes accessed | tf_op | source)
XLA Modules:
  0.0 230.3 jit_solution(12086792770830489114)
XLA Ops:
  12.6 1.5 copy.108
  18.7 2.3 copy.109
  23.3 14.7 %all-reduce = f32[128]{0:T(128)S(1)} all-reduce(f32[128]{0:T(128)S(1)} %dynamic-update-slice), channel_id=3, replica_groups=mesh['dp'=2,'ctx_0'=4,'ctx_1'=8,'tp'=8] {'ctx_1'}, use_global_device_ids=true, to_apply=%add | all-reduce | flops 128 | bytes 1024
  40.6 40.6 %all-gather.8.cloned.1.call-done = f32[128,64,128]{2,1,0:T(8,128)} async-done(((f32[16,64,128]{2,1,0:T(8,128)}), f32[128,64,128]{2,1,0:T(8,128)}) %all-gather.8.cloned.1.call-update) | async-done | bytes 4194320 | tf_op jit(solution)/shard_map/all_gather | solution.py:29
  81.2 3.3 %bitcast_add_fusion.11 = f32[1,16,64,128]{3,2,1,0:T(8,128)} fusion(f32[128,64,128]{2,1,0:T(8,128)} %all-gather.8.cloned.1.call-done, f32[16]{0:T(128)} %get-tuple-element.283, f32[16]{0:T(128)} %get-tuple-element.285, f32[16]{0:T(128)} %get-tuple-element.286, f32[16]{0:T(128)} %get-tuple-element.287, f32[16]{0:T(128)} %get-tuple-element.288, ...), kind=kLoop, calls=%fused_computation.64 | loop fusion | flops 1966080 | bytes 4719104 | tf_op jit(solution)/shard_map/add | solution.py:115
  85.2 1.7 broadcast_in_dim.91
  86.8 33.6 %while.18 = (s32[]{:T(128)}, f32[512,512]{1,0:T(8,128)S(1)}, f32[512,16,64]{0,2,1:T(8,128)}, f32[16,512]{1,0:T(8,128)}, f32[16,512]{1,0:T(8,128)S(1)}, /*index=5...) while((s32[]{:T(128)}, f32[512,512]{1,0:T(8,128)S(1)}, ...), condition=%wide.region_8.9_spmd.clone, body=%wide.region_4.8_spmd.clone.sunk | while | flops 285210624 | bytes 12701929 | solution.py:111
  87.8 3.8 %fusion.88 = (f32[4,512]{1,0:T(4,128)S(1)}, f32[4,512]{1,0:T(4,128)S(1)}, f32[512,512]{1,0:T(8,128)S(1)}) fusion(f32[512,512]{1,0:T(8,128)} %get-tuple-element.397, f32[4,512]{1,0:T(4,128)S(1)} %get-tuple-element.356, f32[4,512]{1,0:T(4,128)S(1)} %get-tuple-element.357, pred[512,512]{1,0:T(8,128)(4,1)S(1)} %fusion.87, ...), kind=kOutput, calls=%fused_computation.6.clone.1 | convolution fusion | flops 144437248 | bytes 2925568 | tf_op jit(solution)/shard_map/while/body/eval_jaxpr/ihp,jhp->hij/dot_general | solution.py:95
  92.8 2.5 %fusion.89 = f32[512,16,64]{0,2,1:T(8,128)} fusion(f32[512,16,64]{0,2,1:T(8,128)} %get-tuple-element.377, s32[]{:T(128)S(6)} %select_n.493, f32[512,512]{1,0:T(8,128)S(1)} %copy-done.8, f32[4,512]{1,0:T(4,128)S(1)} %get-tuple-element.357, pred[512,512]{1,0:T(8,128)(4,1)S(1)} %fusion.87, bf16[512,16,64]{0,2,1:T(8,128)(2,1)S(1)} %get-tuple-element.394), kind=kOutput, calls=%fused_computation.11.clone.1 | convolution fusion | flops 139460608 | bytes 2114560 | tf_op jit(solution)/shard_map/while/body/eval_jaxpr/hij,ihp->jhp/dot_general | solution.py:98
  96.2 3.8 %fusion.88 = (f32[4,512]{1,0:T(4,128)S(1)}, f32[4,512]{1,0:T(4,128)S(1)}, f32[512,512]{1,0:T(8,128)S(1)}) fusion(f32[512,512]{1,0:T(8,128)} %get-tuple-element.397, f32[4,512]{1,0:T(4,128)S(1)} %get-tuple-element.356, f32[4,512]{1,0:T(4,128)S(1)} %get-tuple-element.357, pred[512,512]{1,0:T(8,128)(4,1)S(1)} %fusion.87, ...), kind=kOutput, calls=%fused_computation.6.clone.1 | convolution fusion | flops 144437248 | bytes 2925568 | tf_op jit(solution)/shard_map/while/body/eval_jaxpr/ihp,jhp->hij/dot_general | solution.py:95
  101.2 2.5 %fusion.89 = f32[512,16,64]{0,2,1:T(8,128)} fusion(f32[512,16,64]{0,2,1:T(8,128)} %get-tuple-element.377, s32[]{:T(128)S(6)} %select_n.493, f32[512,512]{1,0:T(8,128)S(1)} %copy-done.8, f32[4,512]{1,0:T(4,128)S(1)} %get-tuple-element.357, pred[512,512]{1,0:T(8,128)(4,1)S(1)} %fusion.87, bf16[512,16,64]{0,2,1:T(8,128)(2,1)S(1)} %get-tuple-element.394), kind=kOutput, calls=%fused_computation.11.clone.1 | convolution fusion | flops 139460608 | bytes 2114560 | tf_op jit(solution)/shard_map/while/body/eval_jaxpr/hij,ihp->jhp/dot_general | solution.py:98
  104.7 3.8 %fusion.88 = (f32[4,512]{1,0:T(4,128)S(1)}, f32[4,512]{1,0:T(4,128)S(1)}, f32[512,512]{1,0:T(8,128)S(1)}) fusion(f32[512,512]{1,0:T(8,128)} %get-tuple-element.397, f32[4,512]{1,0:T(4,128)S(1)} %get-tuple-element.356, f32[4,512]{1,0:T(4,128)S(1)} %get-tuple-element.357, pred[512,512]{1,0:T(8,128)(4,1)S(1)} %fusion.87, ...), kind=kOutput, calls=%fused_computation.6.clone.1 | convolution fusion | flops 144437248 | bytes 2925568 | tf_op jit(solution)/shard_map/while/body/eval_jaxpr/ihp,jhp->hij/dot_general | solution.py:95
  109.7 2.4 %fusion.89 = f32[512,16,64]{0,2,1:T(8,128)} fusion(f32[512,16,64]{0,2,1:T(8,128)} %get-tuple-element.377, s32[]{:T(128)S(6)} %select_n.493, f32[512,512]{1,0:T(8,128)S(1)} %copy-done.8, f32[4,512]{1,0:T(4,128)S(1)} %get-tuple-element.357, pred[512,512]{1,0:T(8,128)(4,1)S(1)} %fusion.87, bf16[512,16,64]{0,2,1:T(8,128)(2,1)S(1)} %get-tuple-element.394), kind=kOutput, calls=%fused_computation.11.clone.1 | convolution fusion | flops 139460608 | bytes 2114560 | tf_op jit(solution)/shard_map/while/body/eval_jaxpr/hij,ihp->jhp/dot_general | solution.py:98
  113.0 3.8 %fusion.88 = (f32[4,512]{1,0:T(4,128)S(1)}, f32[4,512]{1,0:T(4,128)S(1)}, f32[512,512]{1,0:T(8,128)S(1)}) fusion(f32[512,512]{1,0:T(8,128)} %get-tuple-element.397, f32[4,512]{1,0:T(4,128)S(1)} %get-tuple-element.356, f32[4,512]{1,0:T(4,128)S(1)} %get-tuple-element.357, pred[512,512]{1,0:T(8,128)(4,1)S(1)} %fusion.87, ...), kind=kOutput, calls=%fused_computation.6.clone.1 | convolution fusion | flops 144437248 | bytes 2925568 | tf_op jit(solution)/shard_map/while/body/eval_jaxpr/ihp,jhp->hij/dot_general | solution.py:95
  118.0 2.4 %fusion.89 = f32[512,16,64]{0,2,1:T(8,128)} fusion(f32[512,16,64]{0,2,1:T(8,128)} %get-tuple-element.377, s32[]{:T(128)S(6)} %select_n.493, f32[512,512]{1,0:T(8,128)S(1)} %copy-done.8, f32[4,512]{1,0:T(4,128)S(1)} %get-tuple-element.357, pred[512,512]{1,0:T(8,128)(4,1)S(1)} %fusion.87, bf16[512,16,64]{0,2,1:T(8,128)(2,1)S(1)} %get-tuple-element.394), kind=kOutput, calls=%fused_computation.11.clone.1 | convolution fusion | flops 139460608 | bytes 2114560 | tf_op jit(solution)/shard_map/while/body/eval_jaxpr/hij,ihp->jhp/dot_general | solution.py:98
  120.5 3.0 %bitcast_multiply_fusion = f32[1,512,1024]{1,2,0:T(8,128)} fusion(bf16[1,512,1024]{1,2,0:T(8,128)(2,1)} %bitcast.282, f32[512,16]{0,1:T(8,128)} %get-tuple-element.268), kind=kLoop, calls=%fused_computation.29 | loop fusion | flops 1048576 | bytes 3178496 | tf_op jit(solution)/shard_map/mul | solution.py:177
  123.5 7.8 %all-gather.2 = f32[4,1,16]{2,1,0:T(1,128)S(1)} all-gather(f32[1,1,16]{2,1,0:T(1,128)S(1)} %fusion.71), channel_id=1, replica_groups=mesh['dp'=2,'ctx_0'=4,'ctx_1'=8,'tp'=8] {'ctx_0'}, dimensions={0}, use_global_device_ids=true | all-gather | bytes 320 | tf_op jit(solution)/shard_map/all_gather | solution.py:29
  134.0 4.0 %fusion.34 = f32[16]{0:T(128)S(1)} fusion(f32[1,1,16,64,128]{4,3,2,1,0:T(8,128)} %param.15, f32[4,16,64,128]{3,2,1,0:T(8,128)} %all-gather.6.cloned.1.call-done, f32[128,64,128]{2,1,0:T(8,128)} %all-gather.8.cloned.1.call-done, f32[16]{0:T(128)S(1)} %get-tuple-element.279, f32[16]{0:T(128)S(1)} %get-tuple-element.277, f32[16]{0:T(128)S(1)} %get-tuple-element.278, ...), kind=kLoop, calls=%fused_computation.51 | loop fusion | flops 4980720 | bytes 6816652 | tf_op jit(solution)/shard_map/reduce_sum | solution.py:185
  138.1 3.9 %multiply_add_fusion = f32[1,16,64,128]{3,2,1,0:T(8,128)S(1)} fusion(f32[4,16,64,128]{3,2,1,0:T(8,128)} %all-gather.6.cloned.1.call-done, f32[128,64,128]{2,1,0:T(8,128)} %all-gather.8.cloned.1.call-done, f32[16]{0:T(128)S(1)} %copy-done.16, f32[16]{0:T(128)S(1)} %copy-done.18, f32[16]{0:T(128)S(1)} %copy-done.19, f32[16]{0:T(128)S(1)} %copy-done.20, ...), kind=kLoop, calls=%fused_computation.65 | loop fusion | flops 4718592 | bytes 6816588 | tf_op jit(solution)/shard_map/add | solution.py:115
  142.1 2.9 %fusion.25 = (f32[16,512]{1,0:T(8,128)S(1)}, f32[16,512]{1,0:T(8,128)S(1)}, f32[16,64,512]{2,1,0:T(8,128)}) fusion(bf16[16,512,64]{1,2,0:T(8,128)(2,1)S(1)} %bitcast.283, f32[512,16]{0,1:T(8,128)S(1)} %get-tuple-element.269, f32[512,16,64]{0,2,1:T(8,128)S(1)} %copy-done.1, bf16[1,512,256]{2,1,0:T(8,128)(2,1)S(1)} %copy-done.7, ...), kind=kOutput, calls=%fused_computation.28 | convolution fusion | flops 808960000 | bytes 5996544 | tf_op jit(solution)/shard_map/jn,hpn->jhp/dot_general | solution.py:172
  148.8 7.1 %all-to-all-start = ((bf16[8,16,512]{2,1,0:T(8,128)(2,1)}), bf16[8,16,512]{2,1,0:T(8,128)(2,1)S(1)}, u32[]{:S(2)}, u32[]{:S(2)}) async-start(bf16[8,16,512]{2,1,0:T(8,128)(2,1)} %broadcast_in_dim.97), calls=%async_computation | async-start | bytes 262144 | tf_op jit(solution)/shard_map/all_to_all | solution.py:47
  155.8 1.4 convolution_add_fusion
  157.3 6.6 %all-to-all-done = bf16[8,16,512]{2,1,0:T(8,128)(2,1)S(1)} async-done(((bf16[8,16,512]{2,1,0:T(8,128)(2,1)}), bf16[8,16,512]{2,1,0:T(8,128)(2,1)S(1)}, u32[]{:S(2)}, u32[]{:S(2)}) %all-to-all-start) | async-done | bytes 131104 | tf_op jit(solution)/shard_map/all_to_all | solution.py:47
  165.5 9.8 %all-to-all-start.1 = ((f32[64,2,1024]{2,1,0:T(2,128)}), f32[64,2,1024]{2,1,0:T(2,128)}, u32[]{:S(2)}, u32[]{:S(2)}) async-start(f32[64,2,1024]{2,1,0:T(2,128)} %copy.117), calls=%async_computation.1 | async-start | bytes 1048576 | tf_op jit(solution)/shard_map/all_to_all | solution.py:62
  175.3 3.1 %convolution_bitcast_fusion = f32[512,128]{0,1:T(8,128)S(1)} fusion(f32[512,16,64]{0,2,1:T(8,128)} %bitcast.286, f32[1,16,64,128]{3,2,1,0:T(8,128)S(1)} %multiply_add_fusion), kind=kOutput, calls=%fused_computation.36 | convolution fusion | flops 805306368 | bytes 2883584 | tf_op jit(solution)/shard_map/jhp,hpn->jn/dot_general | solution.py:178
  179.8 2.0 copy.143
  181.8 12.0 %all-to-all-done.1 = f32[64,2,1024]{2,1,0:T(2,128)} async-done(((f32[64,2,1024]{2,1,0:T(2,128)}), f32[64,2,1024]{2,1,0:T(2,128)}, u32[]{:S(2)}, u32[]{:S(2)}) %all-to-all-start.1) | async-done | bytes 524320 | tf_op jit(solution)/shard_map/all_to_all | solution.py:62
  195.2 9.0 %all_to_all.22 = f32[8,1,2]{2,1,0:T(1,128)S(1)} all-to-all(f32[8,1,2]{2,1,0:T(1,128)S(1)} %broadcast_in_dim.98), channel_id=1, replica_groups=mesh['dp'=2,'ctx_0'=4,'ctx_1'=8,'tp'=8] {'tp'}, dimensions={0} | all-to-all | bytes 128 | tf_op jit(solution)/shard_map/all_to_all | solution.py:47
  206.1 6.6 %all-to-all-start.3 = ((f32[64,1,1]{2,1,0:T(1,128)}), f32[64,1,1]{2,1,0:T(1,128)S(1)}, u32[]{:S(2)}, u32[]{:S(2)}) async-start(f32[64,1,1]{2,1,0:T(1,128)} %broadcast_in_dim.99), calls=%async_computation.3 | async-start | bytes 65536 | tf_op jit(solution)/shard_map/all_to_all | solution.py:47
  212.8 3.2 %multiply_convert_fusion = bf16[512,16,64]{0,2,1:T(8,128)(2,1)} fusion(f32[512,16]{0,1:T(8,128)S(1)} %copy-done.15, f32[512,16,64]{0,2,1:T(8,128)S(1)} %copy-done.2, f32[16,64,512]{2,1,0:T(8,128)} %get-tuple-element.289, f32[512,16]{0,1:T(8,128)S(1)} %copy-done.13), kind=kLoop, calls=%fused_computation.34 | loop fusion | flops 2097152 | bytes 5308416 | tf_op jit(solution)/shard_map/convert_element_type | solution.py:181
  215.9 2.3 copy.120
  219.9 1.9 all-to-all-done.3
  (143 shorter events, 38.6 us)
Async XLA Ops:
  7.2 156.8 %copy-start = (bf16[1,512,1024]{2,1,0:T(8,128)(2,1)S(1)}, bf16[1,512,1024]{2,1,0:T(8,128)(2,1)}, u32[]{:S(2)}) copy-start(bf16[1,512,1024]{2,1,0:T(8,128)(2,1)} %param.16) | copy-start | bytes 3145732
  7.2 8.3 %copy-start.11 = (f32[1,16,512]{2,1,0:T(8,128)S(1)}, f32[1,16,512]{2,1,0:T(8,128)}, u32[]{:S(2)}) copy-start(f32[1,16,512]{2,1,0:T(8,128)} %param.13) | copy-start | bytes 98308
  7.2 74.0 %all-gather.8.cloned.1.call-start = ((), (), s32[]{:S(2)}) async-start(), calls=%async_computation.6 | async-start | bytes 4718592 | tf_op jit(solution)/shard_map/all_gather | solution.py:29
  8.0 6.8 %copy-start.23 = (f32[16]{0:T(128)}, f32[16]{0:T(128)S(1)}, u32[]{:S(2)}) copy-start(f32[16]{0:T(128)S(1)} %exponential_negate_fusion) | copy-start | bytes 196
  12.6 4.8 %copy-start.7 = (bf16[1,512,256]{2,1,0:T(8,128)(2,1)S(1)}, bf16[1,512,256]{2,1,0:T(8,128)(2,1)}, u32[]{:S(2)}) copy-start(bf16[1,512,256]{2,1,0:T(8,128)(2,1)} %param.12) | copy-start | bytes 786436
  16.2 125.8 %copy-start.12 = (f32[512,16]{0,1:T(8,128)}, f32[512,16]{0,1:T(8,128)S(1)}, u32[]{:S(2)}) copy-start(f32[512,16]{0,1:T(8,128)S(1)} %get-tuple-element.269) | copy-start | bytes 98308
  18.6 115.3 %all-gather.6.cloned.1.call-start = ((), (), s32[]{:S(2)}) async-start(), calls=%async_computation.5 | async-start | bytes 2621440 | tf_op jit(solution)/shard_map/all_gather | solution.py:29
  91.5 1.2 copy-start.8
  99.9 1.3 copy-start.8
  108.4 1.2 copy-start.8
  120.5 10.9 %copy-start.5 = (bf16[1,512,1024]{1,2,0:T(8,128)(2,1)S(1)}, bf16[1,512,1024]{1,2,0:T(8,128)(2,1)}, u32[]{:S(2)}) copy-start(bf16[1,512,1024]{1,2,0:T(8,128)(2,1)} %copy-done.4) | copy-start | bytes 3145732
  120.5 10.9 %copy-start.6 = (f32[1,1,16,64,128]{4,3,2,1,0:T(8,128)S(1)}, f32[1,1,16,64,128]{4,3,2,1,0:T(8,128)}, u32[]{:S(2)}) copy-start(f32[1,1,16,64,128]{4,3,2,1,0:T(8,128)} %param.15) | copy-start | bytes 1572868
  133.9 4.1 %copy-start.16 = (f32[16]{0:T(128)S(1)}, f32[16]{0:T(128)}, u32[]{:S(2)}) copy-start(f32[16]{0:T(128)} %get-tuple-element.283) | copy-start | bytes 196
  133.9 4.1 %copy-start.17 = (f32[16]{0:T(128)S(1)}, f32[16]{0:T(128)}, u32[]{:S(2)}) copy-start(f32[16]{0:T(128)} %get-tuple-element.284) | copy-start | bytes 196
  133.9 4.1 %copy-start.18 = (f32[16]{0:T(128)S(1)}, f32[16]{0:T(128)}, u32[]{:S(2)}) copy-start(f32[16]{0:T(128)} %get-tuple-element.285) | copy-start | bytes 196
  133.9 4.1 %copy-start.19 = (f32[16]{0:T(128)S(1)}, f32[16]{0:T(128)}, u32[]{:S(2)}) copy-start(f32[16]{0:T(128)} %get-tuple-element.286) | copy-start | bytes 196
  133.9 4.1 %copy-start.20 = (f32[16]{0:T(128)S(1)}, f32[16]{0:T(128)}, u32[]{:S(2)}) copy-start(f32[16]{0:T(128)} %get-tuple-element.287) | copy-start | bytes 196
  133.9 4.1 %copy-start.21 = (f32[16]{0:T(128)S(1)}, f32[16]{0:T(128)}, u32[]{:S(2)}) copy-start(f32[16]{0:T(128)} %get-tuple-element.288) | copy-start | bytes 196
  133.9 4.1 %copy-start.22 = (f32[16]{0:T(128)S(1)}, f32[16]{0:T(128)}, u32[]{:S(2)}) copy-start(f32[16]{0:T(128)} %get-tuple-element.280) | copy-start | bytes 196
  138.1 3.9 %copy-start.1 = (f32[512,16,64]{0,2,1:T(8,128)S(1)}, f32[512,16,64]{0,2,1:T(8,128)}, u32[]{:S(2)}) copy-start(f32[512,16,64]{0,2,1:T(8,128)} %get-tuple-element.174) | copy-start | bytes 6291460
  138.1 3.9 %copy-start.3 = (bf16[512,16,64]{0,2,1:T(8,128)(2,1)S(1)}, bf16[512,16,64]{0,2,1:T(8,128)(2,1)}, u32[]{:S(2)}) copy-start(bf16[512,16,64]{0,2,1:T(8,128)(2,1)} %get-tuple-element.408) | copy-start | bytes 3145732
  142.0 3.3 %copy-start.14 = (f32[16,512]{1,0:T(8,128)S(1)}, f32[16,512]{1,0:T(8,128)}, u32[]{:S(2)}) copy-start(f32[16,512]{1,0:T(8,128)} %get-tuple-element.176) | copy-start | bytes 98308
  142.0 5.4 %copy-start.24 = (f32[16]{0:T(128)S(1)}, f32[16]{0:T(128)}, u32[]{:S(2)}) copy-start(f32[16]{0:T(128)} %copy-done.23) | copy-start | bytes 196
  142.1 13.8 %copy-start.9 = (f32[512,128]{0,1:T(8,128)S(1)}, f32[512,128]{0,1:T(8,128)}, u32[]{:S(2)}) copy-start(f32[512,128]{0,1:T(8,128)} %convolution_bitcast_fusion.1) | copy-start | bytes 786436
  148.8 15.1 %all-to-all-start = ((bf16[8,16,512]{2,1,0:T(8,128)(2,1)}), bf16[8,16,512]{2,1,0:T(8,128)(2,1)S(1)}, u32[]{:S(2)}, u32[]{:S(2)}) async-start(bf16[8,16,512]{2,1,0:T(8,128)(2,1)} %broadcast_in_dim.97), calls=%async_computation | async-start | bytes 262144 | tf_op jit(solution)/shard_map/all_to_all | solution.py:47
  165.5 28.4 %all-to-all-start.1 = ((f32[64,2,1024]{2,1,0:T(2,128)}), f32[64,2,1024]{2,1,0:T(2,128)}, u32[]{:S(2)}, u32[]{:S(2)}) async-start(f32[64,2,1024]{2,1,0:T(2,128)} %copy.117), calls=%async_computation.1 | async-start | bytes 1048576 | tf_op jit(solution)/shard_map/all_to_all | solution.py:62
  175.3 42.9 %reduce-scatter.4.cloned.1.call-start = ((), (), s32[]{:S(2)}) async-start(), calls=%async_computation.7 | async-start | bytes 589824
  175.3 3.6 %copy-start.10 = (f32[512,128]{0,1:T(8,128)S(1)}, f32[512,128]{0,1:T(8,128)}, u32[]{:S(2)}) copy-start(f32[512,128]{0,1:T(8,128)} %convolution_add_fusion) | copy-start | bytes 786436
  178.4 34.3 %copy-start.13 = (f32[512,16]{0,1:T(8,128)S(1)}, f32[512,16]{0,1:T(8,128)}, u32[]{:S(2)}) copy-start(f32[512,16]{0,1:T(8,128)} %copy-done.12) | copy-start | bytes 98308
  178.4 34.3 %copy-start.15 = (f32[512,16]{0,1:T(8,128)S(1)}, f32[512,16]{0,1:T(8,128)}, u32[]{:S(2)}) copy-start(f32[512,16]{0,1:T(8,128)} %get-tuple-element.271) | copy-start | bytes 98308
  178.9 33.8 %copy-start.2 = (f32[512,16,64]{0,2,1:T(8,128)S(1)}, f32[512,16,64]{0,2,1:T(8,128)}, u32[]{:S(2)}) copy-start(f32[512,16,64]{0,2,1:T(8,128)} %get-tuple-element.174) | copy-start | bytes 6291460
  206.1 15.7 %all-to-all-start.3 = ((f32[64,1,1]{2,1,0:T(1,128)}), f32[64,1,1]{2,1,0:T(1,128)S(1)}, u32[]{:S(2)}, u32[]{:S(2)}) async-start(f32[64,1,1]{2,1,0:T(1,128)} %broadcast_in_dim.99), calls=%async_computation.3 | async-start | bytes 65536 | tf_op jit(solution)/shard_map/all_to_all | solution.py:47
  (2 other events, 2.2 us)
Sparse Core Ops, SparseCore 0:
  18.7 62.4 all-gather.7
  84.7 35.0 all-gather.5
  182.0 31.7 reduce-scatter.3
where the time goes:
time: 232 us; the launch traced here: 230 us
  waiting for transfers between devices  61.2 us (26%)
  matrix products  38.1 us (16%)
  other arithmetic  34.4 us (15%)
  blocking collectives  31.5 us (14%)
  local copies, waits for them, and re-layouts  25.3 us (11%)
  starting transfers between devices  23.6 us (10%)
  between operations  16.2 us (7%)
    all_gather x2, waiting for transfers between devices, carried_in(): pieces = jax.tree.map(lambda part: lax.all_gather(part, axis), subtotal)  40.6 us
    dot_general x4, matrix products, one_group(): jnp.einsum('ihp,jhp->hij', y_part, x_part, preferred_element_type=jnp.flo...  15.1 us
    unnamed x1, blocking collectives  14.7 us
    all_to_all x2, starting transfers between devices, sent_to_all(): return lax.all_to_all(copies, axis, split_axis=0, concat_axis=0, tiled=True)  13.7 us
    unnamed x57, local copies, waits for them, and re-layouts  12.3 us
    all_to_all x1, waiting for transfers between devices, summed_on_arrival(): blocks = lax.all_to_all(in_blocks(x, dim, count), axis, 0, 0, tiled=True)  12 us
    dot_general x4, matrix products, one_group(): jnp.einsum('hij,ihp->jhp', rounded, y_part, preferred_element_type=jnp.fl...  9.79 us
    all_to_all x1, starting transfers between devices, summed_on_arrival(): blocks = lax.all_to_all(in_blocks(x, dim, count), axis, 0, 0, tiled=True)  9.77 us
  transfers between devices with their start and end apart: 6, of which 4 were waited for; matrix products, arithmetic and copies ran while one was open for 28% of the time, Pallas kernels for 0%

commit v1 on v0

v1 whole, which is shorter than its diff:
```python
import jax
import jax.numpy as jnp
from jax import lax
from jax.experimental import pallas as pl
from jax.experimental.pallas import tpu as pltpu
from jax.sharding import Mesh
from jax.sharding import PartitionSpec as P

HEAD_DIM = 64
STATE = 128
SUB = 128
CTX = ("ctx_0", "ctx_1")
DP_CTX = ("dp", "ctx_0", "ctx_1")
CTX_TP = ("ctx_0", "ctx_1", "tp")
epsilon = 1e-06
NEG = -1e30

f32 = jnp.float32
bf16 = jnp.bfloat16
VMEM = pl.BlockSpec(memory_space=pltpu.VMEM)
SMEM = pl.BlockSpec(memory_space=pltpu.SMEM)


def dot(a, b, ca, cb):
    return lax.dot_general(a, b, (((ca,), (cb,)), ((), ())), preferred_element_type=f32)


def iota(shape, dim):
    return lax.broadcasted_iota(jnp.int32, shape, dim)


def doc_ends(docs):
    ends, total = [], 0
    for k in range(docs.shape[1]):
        total = total + docs[0, k]
        ends.append(total)
    return ends


def label_of(position, ends):
    label = 0
    for end in ends:
        label = label + jnp.where(position >= end, 1, 0)
    return label


def label_before(anchor, ends):
    return jnp.where(anchor > 0, label_of(anchor - 1, ends), -1)


def running(x, reverse=False):
    length = x.shape[1]
    lane = iota(x.shape, 1)
    step = 1
    while step < length:
        if reverse:
            x = x + jnp.where(lane < length - step, pltpu.roll(x, length - step, 1), 0.0)
        else:
            x = x + jnp.where(lane >= step, pltpu.roll(x, step, 1), 0.0)
        step *= 2
    return x


def steps_of(raw, a_log, heads):
    step = jnp.maximum(raw, 0.0) + jnp.log1p(jnp.exp(-jnp.abs(raw)))
    row = iota((heads, 1), 0)
    column = jnp.zeros((heads, 1), f32)
    for h in range(heads):
        column = jnp.where(row == h, a_log[h], column)
    rate = jnp.exp(column)
    return step, rate, -running(rate * step)


def split_two(x):
    high = x.astype(bf16)
    return high, (x - high.astype(f32)).astype(bf16)


def tall(x):
    high = x.astype(bf16).astype(f32)
    return jnp.transpose(jnp.concatenate([high, x - high], axis=0)).astype(bf16)


def spread_matrix(heads):
    shape = (2 * heads, heads * HEAD_DIM)
    return jnp.where(iota(shape, 1) // HEAD_DIM == iota(shape, 0) % heads, 1.0, 0.0).astype(bf16)


def gather_matrix(heads):
    shape = (heads, heads * HEAD_DIM)
    return jnp.where(iota(shape, 1) // HEAD_DIM == iota(shape, 0), 1.0, 0.0).astype(bf16)


def first_kernel(docs, anchor, a_log, raw, dy, maps, out):
    heads, length = raw.shape
    ends = doc_ends(docs)
    labels = label_of(anchor[0] + iota((1, length), 1), ends)
    step, rate, cum = steps_of(raw[...], a_log, heads)
    enter = jnp.where(labels == label_before(anchor[0], ends), jnp.exp(cum), 0.0)
    scaled = (dot(tall(enter), spread_matrix(heads), 1, 0) * dy[...].astype(f32)).astype(bf16)
    local = dot(scaled, maps[:, STATE:], 0, 0).astype(bf16)
    last = jnp.broadcast_to(enter[:, length - 1 :], (heads, STATE))
    high = last.astype(bf16).astype(f32)
    low = last - high
    row = iota((8, STATE), 0)
    rows = out.shape[1] - 8
    per_head = HEAD_DIM // rows
    for h in range(heads):
        tail = jnp.where(row == 0, high[h : h + 1], jnp.where(row == 1, low[h : h + 1], 0.0))
        for part in range(per_head):
            start = h * HEAD_DIM + part * rows
            out[h * per_head + part, :rows, :] = local[start : start + rows]
            out[h * per_head + part, rows:, :] = tail.astype(bf16)


def scan_kernel(pieces, out):
    blocks, rows = out.shape[:2]
    carry = jnp.zeros(out.shape[1:], f32)
    for k in reversed(range(blocks)):
        out[k] = carry.astype(bf16)
        if k:
            tail = pieces[k, rows:, :].astype(f32)
            carry = pieces[k, :rows, :].astype(f32) + (tail[0:1] + tail[1:2]) * carry


def quad_kernel(
    docs, anchor, a_log, raw, x, dy, maps, states,
    rdt_out, xl_out, gm_out, vec_out,
    ye, yo, xe, xo, sa, sb, sc, dte, gae, gbe, ua, ub, zs, dd, pb, ms, cum_tall, tl,
):
    heads, length = raw.shape
    wide = x.shape[1]
    half, quarter = length // 2, length // 4
    ends = doc_ends(docs)
    base = anchor[0]
    position = iota((1, length), 1)
    labels = label_of(base + position, ends)
    step, rate, cum = steps_of(raw[...], a_log, heads)
    enter = jnp.where(labels == label_before(base, ends), jnp.exp(cum), 0.0)
    leave = jnp.where(
        labels == label_of(base + length - 1, ends), jnp.exp(cum[:, length - 1 :] - cum), 0.0
    )
    toward_a = jnp.where(position < half, 1.0, -1.0)
    mid = cum[:, half - 1 : half]
    scale_a = jnp.where(
        labels == label_of(base + half - 1, ends), jnp.exp((mid - cum) * toward_a), 0.0
    )
    low_half = position < half
    first = (position // quarter) % 2 == 0
    toward_b = jnp.where(first, 1.0, -1.0)
    edge = jnp.where(
        low_half, cum[:, quarter - 1 : quarter], cum[:, half + quarter - 1 : half + quarter]
    )
    edge_label = jnp.where(
        low_half, label_of(base + quarter - 1, ends), label_of(base + half + quarter - 1, ends)
    )
    scale_b = jnp.where(labels == edge_label, jnp.exp((edge - cum) * toward_b), 0.0)
    cum_tall[...] = jnp.transpose(cum)
    for k, scale in enumerate((step, enter, leave, scale_a, scale_b)):
        tl[k] = tall(scale)

    spread = spread_matrix(heads)
    lane = iota((1, wide), 1)
    even = jnp.where((lane // HEAD_DIM) % 2 == 0, 1.0, 0.0).astype(bf16)
    odd = jnp.where((lane // HEAD_DIM) % 2 == 1, 1.0, 0.0).astype(bf16)

    for d in range(4):
        rows = slice(d * quarter, (d + 1) * quarter)
        yb = dy[rows, :]
        yv = yb.astype(f32)
        dt_e = dot(tl[0, rows, :], spread, 1, 0)
        dte[rows, :] = dt_e
        xdt = (dt_e * x[rows, :].astype(f32)).astype(bf16)
        xv = xdt.astype(f32)
        xe[rows, :] = xdt * even
        xo[rows, :] = xdt * odd
        ye[rows, :] = yb * even
        yo[rows, :] = yb * odd
        sc[rows, :] = (dot(tl[1, rows, :], spread, 1, 0) * yv).astype(bf16)
        xl_out[rows, :] = (dot(tl[2, rows, :], spread, 1, 0) * xv).astype(bf16)
        ga = dot(tl[3, rows, :], spread, 1, 0)
        gb = dot(tl[4, rows, :], spread, 1, 0)
        sa[rows, :] = (ga * (xv if d < 2 else yv)).astype(bf16)
        sb[rows, :] = (gb * (xv if d % 2 == 0 else yv)).astype(bf16)
        if d < 2:
            gae[rows, :] = ga
        if d % 2 == 0:
            gbe[rows, :] = gb

    ms[...] = jnp.zeros(ms.shape, bf16)
    lower, upper = slice(0, half), slice(half, length)
    cba = dot(maps[upper, STATE:], maps[lower, :STATE], 1, 1).astype(bf16)
    ua[lower, :] = dot(cba, sa[upper, :], 0, 0)
    ua[upper, :] = dot(cba, sa[lower, :], 1, 0)
    ms[upper, lower] = dot(sa[upper, :], sa[lower, :], 1, 1).astype(bf16)
    for q in range(2):
        lower = slice(2 * q * quarter, (2 * q + 1) * quarter)
        upper = slice((2 * q + 1) * quarter, (2 * q + 2) * quarter)
        cbb = dot(maps[upper, STATE:], maps[lower, :STATE], 1, 1).astype(bf16)
        ub[lower, :] = dot(cbb, sb[upper, :], 0, 0)
        ub[upper, :] = dot(cbb, sb[lower, :], 1, 0)
        ms[upper, lower] = dot(sb[upper, :], sb[lower, :], 1, 1).astype(bf16)
    sv = states[...].astype(bf16)
    zs[...] = dot(maps[:, STATE:], sv, 1, 1)

    ri, rj = iota((quarter, quarter), 0), iota((quarter, quarter), 1)
    for d in range(4):
        rows = slice(d * quarter, (d + 1) * quarter)
        at = base + d * quarter
        keep = (ri >= rj) & (label_of(at + ri, ends) == label_of(at + rj, ends))
        cb = dot(maps[rows, STATE:], maps[rows, :STATE], 1, 1)
        mask = jnp.where(keep, 0.0, NEG)
        total = jnp.zeros((quarter, quarter), f32)
        for pair in range(heads // 2):
            cols = slice(pair * 2 * HEAD_DIM, (pair + 1) * 2 * HEAD_DIM)
            y2 = jnp.concatenate([ye[rows, cols], yo[rows, cols]], axis=0)
            x2 = jnp.concatenate([xe[rows, cols], xo[rows, cols]], axis=0)
            xp = xe[rows, cols] + xo[rows, cols]
            inner = dot(y2, xp, 1, 1)
            weights = []
            for s in range(2):
                h = 2 * pair + s
                gap = cum_tall[rows, h : h + 1] - cum[h : h + 1, rows]
                kernel = jnp.exp(gap + mask)
                total = total + kernel * inner[s * quarter : (s + 1) * quarter]
                weights.append((kernel * cb).astype(bf16))
            r = dot(jnp.concatenate(weights, axis=0), y2, 0, 0)
            o = dot(jnp.concatenate(weights, axis=1), x2, 1, 0)
            yv = dy[rows, cols].astype(f32)
            back = xp.astype(f32) * r
            fore = yv * o + sc[rows, cols].astype(f32) * zs[rows, cols]
            ta = sa[rows, cols].astype(f32) * ua[rows, cols]
            tb = sb[rows, cols].astype(f32) * ub[rows, cols]
            if d < 2:
                back = back + ta
                r = r + gae[rows, cols] * ua[rows, cols]
            else:
                fore = fore + ta
            if d % 2 == 0:
                back = back + tb
                r = r + gbe[rows, cols] * ub[rows, cols]
            else:
                fore = fore + tb
            rdt_out[rows, cols] = dte[rows, cols] * r
            pb[rows, cols] = back.astype(bf16)
            dd[rows, cols] = fore - back
        ms[rows, rows] = total.astype(bf16)

    collect = gather_matrix(heads)
    high, low = split_two(dd[...])
    dc = dot(collect, high, 1, 1) + dot(collect, low, 1, 1)
    b0 = dot(collect, pb[...], 1, 1)
    tail = running(dc, reverse=True)
    sig = 1.0 / (1.0 + jnp.exp(-raw[...]))
    over = sig / step
    turn = rate * sig
    vec_out[0] = b0 * over - turn * tail
    vec_out[1] = over
    vec_out[2] = turn
    vec_out[3] = step * leave
    vec_out[4] = jnp.broadcast_to(enter[:, length - 1 :], (heads, length))
    gm_out[:, :STATE] = dot(ms[...], maps[:, STATE:], 0, 0)
    gm_out[:, STATE:] = dot(ms[...], maps[:, :STATE], 1, 0) + dot(sc[...], sv, 1, 0)


def step_kernel(maps, carry, xl, states, vec, out, order):
    heads, length = vec.shape[1:]
    collect = gather_matrix(heads)
    both = carry[...].astype(f32) * states[...]
    inside = jnp.sum(both.reshape(heads, HEAD_DIM, STATE), axis=1)
    v = vec[4, :, 0:1] * jnp.sum(inside, axis=1, keepdims=True)
    got = []
    part = length // 4
    for d in range(4):
        rows = slice(d * part, (d + 1) * part)
        cb = dot(maps[rows, :STATE], carry[...], 1, 1)
        got.append(dot(collect, (xl[rows, :].astype(f32) * cb).astype(bf16), 1, 1))
    w = jnp.concatenate(got, axis=1)
    before = running(w) - w
    grad = vec[0] + w * vec[1] - vec[2] * (v + before)
    halves = [[], []]
    for c in range(order.shape[0]):
        order[c] = grad[:, c * 128 : (c + 1) * 128]
        for r in range(2):
            halves[r].append(order[c, pl.ds(r, heads // 2, stride=2), :])
    grad = jnp.concatenate([jnp.concatenate(h, axis=1) for h in halves], axis=0).astype(bf16)
    for k in range(out.shape[0]):
        out[k] = grad


def rest_kernel(maps, carry, xl, rdt, vec, gm, gx_out, gm_out):
    heads, length = vec.shape[1:]
    spread = spread_matrix(heads)
    scale = tall(vec[3])
    part = length // 4
    per = part // gm_out.shape[1]
    for d in range(4):
        rows = slice(d * part, (d + 1) * part)
        cb = dot(maps[rows, :STATE], carry[...], 1, 1)
        gx_out[rows, :] = (
            rdt[rows, :] + dot(scale[rows], spread, 1, 0) * cb
        ).astype(bf16)
        extra = gm[rows, :STATE] + dot(xl[rows, :], carry[...], 1, 0)
        size = part // per
        for k in range(per):
            inner = slice(k * size, (k + 1) * size)
            gm_out[d * per + k, :, :STATE] = extra[inner].astype(bf16)
            gm_out[d * per + k, :, STATE:] = gm[d * part + k * size : d * part + (k + 1) * size, STATE:].astype(bf16)


def project_kernel(grads, tokens, out, product, lined):
    groups, heads, length = grads.shape
    columns = tokens.shape[1]
    chunks = columns // 128
    half = heads // 2
    product[...] = dot(grads[...].reshape(groups * heads, length), tokens[...], 1, 0)
    for z in range(groups):
        for r in range(2):
            for c in range(chunks):
                lined[pl.ds(z * half * 2 * chunks + 2 * c + r, half, stride=2 * chunks), :] = (
                    product[z * heads + r * half : z * heads + (r + 1) * half, c * 128 : (c + 1) * 128]
                )
    out[...] = lined[...].astype(bf16).reshape(out.shape)


def total_kernel(pieces, sum_out, square_out):
    total = jnp.zeros(pieces.shape[1:], f32)
    for k in range(pieces.shape[0]):
        total = total + pieces[k].astype(f32)
    sum_out[...] = total
    square = total * total
    row = iota(total.shape, 0)
    first = jnp.sum(jnp.where(row % 2 == 0, square, 0.0), axis=(0, 1), keepdims=True)
    second = jnp.sum(jnp.where(row % 2 == 1, square, 0.0), axis=(0, 1), keepdims=True)
    shape = square_out.shape[1:]
    both = jnp.where(iota(shape, 0) % 2 == 0, first, second)
    for k in range(square_out.shape[0]):
        square_out[k] = both


def norm_kernel(squares, norm_out, pair_out):
    total = squares[0]
    for k in range(1, squares.shape[0]):
        total = total + squares[k]
    norm = jnp.sqrt(total + epsilon)
    norm_out[...] = norm
    pair = norm[0:1] + norm[1:2]
    for k in range(pair_out.shape[0]):
        pair_out[k] = pair


def clip_kernel(pairs, norm, summed, out):
    heads = 2 * pairs.shape[0]
    target = jnp.sum(pairs[...], axis=0) / heads
    scale = jnp.minimum(1.0, target / norm[...])
    for c in range(summed.shape[0] // 2):
        for r in range(2):
            k = 2 * c + r
            out[r : r + 1, c * 128 : (c + 1) * 128] = summed[k : k + 1, :] * scale[r : r + 1]


def call(kernel, outs, specs, flops, moved, scratch=(), limit=24, name=None):
    return pl.pallas_call(
        kernel,
        out_shape=outs,
        in_specs=specs,
        out_specs=jax.tree.map(lambda _: VMEM, outs),
        scratch_shapes=scratch,
        cost_estimate=pl.CostEstimate(flops=flops, bytes_accessed=moved, transcendentals=0),
        compiler_params=pltpu.CompilerParams(vmem_limit_bytes=limit << 20),
        name=name,
    )


def shards(x_in, grad_out, state_maps, dt_raw, a_log, saved_states, layer_in, doc_lengths):
    length, wide = x_in.shape[1:]
    heads = a_log.shape[0]
    x, dy, maps, raw = x_in[0], grad_out[0], state_maps[0], dt_raw[0]
    states = saved_states.reshape(wide, STATE)
    anchor = (lax.axis_index(CTX) * length).astype(jnp.int32).reshape(1)
    blocks = lax.axis_size(CTX)
    tp = lax.axis_size("tp")
    groups = lax.axis_size(DP_CTX)
    rows = wide // blocks
    SD = jax.ShapeDtypeStruct

    payload = call(
        first_kernel,
        SD((blocks, rows + 8, STATE), bf16),
        [SMEM, SMEM, SMEM, VMEM, VMEM, VMEM],
        200_000_000, 2_000_000, name="first",
    )(doc_lengths, anchor, a_log, raw, dy, maps)
    pieces = lax.all_to_all(payload, CTX, 0, 0, tiled=True)
    carries = call(
        scan_kernel, SD((blocks, rows, STATE), bf16), [VMEM], 1_000_000, 600_000, name="scan"
    )(pieces)
    carry = lax.all_to_all(carries, CTX, 0, 0, tiled=True).reshape(wide, STATE)

    big = lambda dtype: pltpu.VMEM((length, wide), dtype)
    rdt, xl, gm, vec = call(
        quad_kernel,
        (
            SD((length, wide), f32),
            SD((length, wide), bf16),
            SD((length, 2 * STATE), f32),
            SD((5, heads, length), f32),
        ),
        [SMEM, SMEM, SMEM, VMEM, VMEM, VMEM, VMEM, VMEM],
        4_000_000_000, 8_000_000,
        scratch=[
            *[big(bf16)] * 7,
            *[big(f32)] * 7,
            big(bf16),
            pltpu.VMEM((length, length), bf16),
            pltpu.VMEM((length, heads), f32),
            pltpu.VMEM((5, length, 2 * heads), bf16),
        ],
        limit=56, name="quad",
    )(doc_lengths, anchor, a_log, raw, x, dy, maps, states)

    grads = call(
        step_kernel,
        SD((tp, heads, length), bf16),
        [VMEM] * 5,
        300_000_000, 3_000_000,
        scratch=[pltpu.VMEM((length // 128, heads, 128), f32)],
        name="steps",
    )(maps, carry, xl, states, vec)
    gathered = lax.all_to_all(grads, "tp", 0, 0, tiled=True)
    grad_x, parts = call(
        rest_kernel,
        (SD((length, wide), bf16), SD((tp, length // tp, 2 * STATE), bf16)),
        [VMEM] * 6,
        400_000_000, 6_000_000, name="rest",
    )(maps, carry, xl, rdt, vec, gm)

    chunks = wide // 128
    partial = call(
        project_kernel,
        SD((groups, 2 * chunks, 128), bf16),
        [VMEM] * 2,
        200_000_000, 2_000_000,
        scratch=[pltpu.VMEM((tp * heads, wide), f32), pltpu.VMEM((groups * 2 * chunks, 128), f32)],
        name="project",
    )(gathered, layer_in[0])
    arrived = lax.all_to_all(partial, DP_CTX, 0, 0, tiled=True)
    maps_arrived = lax.all_to_all(parts, "tp", 0, 0, tiled=True)
    grad_maps = jnp.sum(maps_arrived.astype(f32), axis=0)

    summed, squares = call(
        total_kernel,
        (SD((2 * chunks, 128), f32), SD((tp, 8, 128), f32)),
        [VMEM],
        1_000_000, 300_000, name="total",
    )(arrived)
    squares = lax.all_to_all(squares, "tp", 0, 0, tiled=True)
    norm, pairs = call(
        norm_kernel,
        (SD((8, 128), f32), SD((groups, 1, 128), f32)),
        [VMEM],
        10_000, 70_000, name="norm",
    )(squares)
    pairs = lax.all_to_all(pairs, DP_CTX, 0, 0, tiled=True)
    grad_dt_proj = call(
        clip_kernel, SD((2, wide), f32), [VMEM] * 3, 10_000, 50_000, name="clip"
    )(pairs, norm, summed)
    return (grad_x[None], grad_maps[None], grad_dt_proj)


def solution(mesh):
    split = Mesh(
        mesh.devices.reshape(mesh.shape["dp"], 4, 8, mesh.shape["tp"]),
        ("dp", "ctx_0", "ctx_1", "tp"),
    )
    return jax.shard_map(
        shards,
        mesh=split,
        in_specs=(
            P("dp", CTX, "tp"),
            P("dp", CTX, "tp"),
            P("dp", CTX, None),
            P("dp", "tp", CTX),
            P("tp"),
            P("dp", CTX, "tp", None, None),
            P("dp", CTX, "tp"),
            P("dp", None),
        ),
        out_specs=(P("dp", CTX, "tp"), P("dp", CTX_TP, None), P(DP_CTX, "tp")),
        check_vma=False,
    )
```

time: 232 us -> 139 us (0.60)
  waiting for transfers between devices: 61.2 us -> 20.3 us
  matrix products: 38.1 us -> 0 us
  other arithmetic: 34.4 us -> 0.67 us
  blocking collectives: 31.5 us -> 64.9 us
  Pallas kernels: 0 us -> 21 us
  local copies, waits for them, and re-layouts: 25.3 us -> 9.02 us
  between operations: 16.2 us -> 0.77 us
    all_to_all x1 -> x3, blocking collectives: 8.99 us -> 64.9 us  [the longest x1 26.6 us: shards(): arrived = lax.all_to_all(partial, DP_CTX, 0, 0, tiled=True)]
    all_gather x2 -> x0, waiting for transfers between devices: 40.6 us -> none  [carried_in(): pieces = jax.tree.map(lambda part: lax.all_gather(part, axis), subtotal)]
    dot_general x17 -> x0, matrix products: 38.1 us -> none  [the longest x4 15.1 us: one_group(): jnp.einsum('ihp,jhp->hij', y_part, x_part, preferred_element_type=jnp.flo...]
    pallas_call x0 -> x9, Pallas kernels: none -> 21 us  [the longest x1 12.5 us: shards(): call(quad_kernel, (SD((length, wide), f32), SD((length, wide), bf16), SD(...]
    unnamed x1 -> x0, blocking collectives: 14.7 us -> none
    add x9 -> x0, other arithmetic: 8.9 us -> none  [the longest x2 7.19 us: combine(): later[1] + later[0][:, None, None] * earlier[1]]
    all_gather x1 -> x0, blocking collectives: 7.82 us -> none  [carried_in(): pieces = jax.tree.map(lambda part: lax.all_gather(part, axis), subtotal)]
    reduce_sum x9 -> x1, other arithmetic: 7.49 us -> 0.67 us  [shards(): grad_maps = jnp.sum(maps_arrived.astype(f32), axis=0)]
  transfers between devices with their start and end apart: 6 -> 4, of which waited for: 4 -> 3; matrix products, arithmetic and copies ran while one was open for 28% -> 0% of each run, Pallas kernels for 0% -> 11%
where the time goes in v1:
time: 139 us; the launch traced here: 138 us
  blocking collectives  64.9 us (47%)
  starting transfers between devices  21.6 us (16%)
  Pallas kernels  21 us (15%)
  waiting for transfers between devices  20.3 us (15%)
  local copies, waits for them, and re-layouts  9.02 us (6%)
    all_to_all x1, blocking collectives, shards(): arrived = lax.all_to_all(partial, DP_CTX, 0, 0, tiled=True)  26.6 us
    all_to_all x1, blocking collectives, shards(): pieces = lax.all_to_all(payload, CTX, 0, 0, tiled=True)  20.5 us
    all_to_all x1, blocking collectives, shards(): gathered = lax.all_to_all(grads, 'tp', 0, 0, tiled=True)  17.9 us
    pallas_call x1, Pallas kernels, shards(): call(quad_kernel, (SD((length, wide), f32), SD((length, wide), bf16), SD(...  12.5 us
    unnamed x28, local copies, waits for them, and re-layouts  9.02 us
    all_to_all x1, waiting for transfers between devices, shards(): maps_arrived = lax.all_to_all(parts, 'tp', 0, 0, tiled=True)  8.73 us
    all_to_all x1, waiting for transfers between devices, shards(): pairs = lax.all_to_all(pairs, DP_CTX, 0, 0, tiled=True)  8.41 us
    all_to_all x1, starting transfers between devices, shards(): pairs = lax.all_to_all(pairs, DP_CTX, 0, 0, tiled=True)  7.68 us
  transfers between devices with their start and end apart: 4, of which 3 were waited for; matrix products, arithmetic and copies ran while one was open for 0% of the time, Pallas kernels for 11%

profile of v1, /device:TPU:1, one launch (start us, length us, event | category | flops | bytes accessed | tf_op | source)
XLA Modules:
  0.0 138.3 jit_solution(9062476922341901242)
XLA Ops:
  0.6 0.0 copy-start.2
  0.6 0.9 copy-done.2
  1.6 1.2 copy-done.5
  2.8 0.8 copy-done.11
  3.6 0.7 copy-done.12
  4.2 0.7 copy-done.13
  4.9 1.9 %first.1 = bf16[32,40,128]{2,1,0:T(8,128)(2,1)S(1)} custom-call(s32[1,4]{1,0:T(1,128)S(1)} %copy-done.12, s32[1]{0:T(128)} %bitcast.1.anchor, f32[16]{0:T(128)S(1)} %copy-done.13, f32[16,512]{1,0:T(8,128)S(1)} %bitcast.22, bf16[512,1024]{1,0:T(8,128)(2,1)S(1)} %bitcast.17, bf16[512,256]{1,0:T(8,128)(2,1)S(1)} %bitcast.13), custom_call_target="tpu_custom_call" | custom-call | flops 200000000 | bytes 2000000 | tf_op jit(solution)/shard_map/first/pallas_call | solution.py:387
  6.8 20.5 %all_to_all.35.pieces = bf16[32,40,128]{2,1,0:T(8,128)(2,1)S(1)} all-to-all(bf16[32,40,128]{2,1,0:T(8,128)(2,1)S(1)} %first.1), channel_id=1, replica_groups=mesh['dp'=2,'ctx_0'=4,'ctx_1'=8,'tp'=8] {'ctx_0','ctx_1'}, dimensions={0} | all-to-all | bytes 655360 | tf_op jit(solution)/shard_map/all_to_all | solution.py:393
  27.3 0.8 scan.1
  28.1 7.2 %all-to-all-start.1 = ((bf16[32,32,128]{2,1,0:T(8,128)(2,1)}), bf16[32,32,128]{2,1,0:T(8,128)(2,1)S(1)}, u32[]{:S(2)}, u32[]{:S(2)}) async-start(bf16[32,32,128]{2,1,0:T(8,128)(2,1)} %scan.1), calls=%async_computation.1 | async-start | bytes 524288 | tf_op jit(solution)/shard_map/all_to_all | solution.py:397
  35.3 0.0 copy-start.3
  35.3 0.0 copy-start.6
  35.3 12.5 %quad.1 = (f32[512,1024]{1,0:T(8,128)}, bf16[512,1024]{1,0:T(8,128)(2,1)}, f32[512,256]{1,0:T(8,128)}, f32[5,16,512]{2,1,0:T(8,128)}) custom-call(s32[1,4]{1,0:T(1,128)} %docs.3, s32[1]{0:T(128)} %bitcast.1.anchor, f32[16]{0:T(128)} %a_log.3, f32[16,512]{1,0:T(8,128)} %bitcast.21, bf16[512,1024]{1,0:T(8,128)(2,1)} %bitcast.24, bf16[512,1024]{1,0:T(8,128)(2,1)} %bitcast.16, ...), custom_call_target="tpu_custom_call" | custom-call | flops 4000000000 | bytes 8000000 | tf_op jit(solution)/shard_map/quad/pallas_call | solution.py:400
  47.8 1.2 copy-done
  49.0 0.9 copy-done.7
  50.0 1.0 copy-done.10
  51.0 1.3 steps.1
  52.3 17.9 %all_to_all.36.grads = bf16[8,16,512]{2,1,0:T(8,128)(2,1)S(1)} all-to-all(bf16[8,16,512]{2,1,0:T(8,128)(2,1)S(1)} %steps.1), channel_id=1, replica_groups=mesh['dp'=2,'ctx_0'=4,'ctx_1'=8,'tp'=8] {'tp'}, dimensions={0} | all-to-all | bytes 262144 | tf_op jit(solution)/shard_map/all_to_all | solution.py:429
  70.2 0.4 project.1
  70.6 26.6 %all_to_all.37.pieces = bf16[64,16,128]{2,1,0:T(8,128)(2,1)S(1)} all-to-all(bf16[64,16,128]{2,1,0:T(8,128)(2,1)S(1)} %project.1), channel_id=1, replica_groups=mesh['dp'=2,'ctx_0'=4,'ctx_1'=8,'tp'=8] {'dp','ctx_0','ctx_1'}, dimensions={0} | all-to-all | bytes 524288 | tf_op jit(solution)/shard_map/all_to_all | solution.py:446
  97.1 0.8 total.1
  98.0 3.3 %all-to-all-start.5 = ((f32[8,8,128]{2,1,0:T(8,128)}), f32[8,8,128]{2,1,0:T(8,128)S(1)}, u32[]{:S(2)}, u32[]{:S(2)}) async-start(f32[8,8,128]{2,1,0:T(8,128)} %get-tuple-element.19), calls=%async_computation.5 | async-start | bytes 65536 | tf_op jit(solution)/shard_map/all_to_all | solution.py:456
  101.3 1.6 %copy-done.4 = f32[512,1024]{1,0:T(8,128)S(1)} copy-done((f32[512,1024]{1,0:T(8,128)S(1)}, f32[512,1024]{1,0:T(8,128)}, u32[]{:S(2)}) %copy-start.4) | copy-done | bytes 2097176
  102.9 2.0 %rest.1 = (bf16[512,1024]{1,0:T(8,128)(2,1)}, bf16[8,64,256]{2,1,0:T(8,128)(2,1)}) custom-call(bf16[512,256]{1,0:T(8,128)(2,1)S(1)} %bitcast.15, bf16[1024,128]{1,0:T(8,128)(2,1)S(1)} %bitcast.11, bf16[512,1024]{1,0:T(8,128)(2,1)S(1)} %copy-done.1, f32[512,1024]{1,0:T(8,128)S(1)} %copy-done.4, f32[5,16,512]{2,1,0:T(8,128)S(1)} %copy-done.8, ...), custom_call_target="tpu_custom_call" | custom-call | flops 400000000 | bytes 6000000 | tf_op jit(solution)/shard_map/rest/pallas_call | solution.py:430
  104.9 3.2 %all-to-all-done.5.squares = f32[8,8,128]{2,1,0:T(8,128)S(1)} async-done(((f32[8,8,128]{2,1,0:T(8,128)}), f32[8,8,128]{2,1,0:T(8,128)S(1)}, u32[]{:S(2)}, u32[]{:S(2)}) %all-to-all-start.5) | async-done | bytes 32800 | tf_op jit(solution)/shard_map/all_to_all | solution.py:456
  108.1 3.4 %all-to-all-start.2 = ((bf16[8,64,256]{2,1,0:T(8,128)(2,1)}), bf16[8,64,256]{2,1,0:T(8,128)(2,1)S(1)}, u32[]{:S(2)}, u32[]{:S(2)}) async-start(bf16[8,64,256]{2,1,0:T(8,128)(2,1)} %get-tuple-element.18), calls=%async_computation.2 | async-start | bytes 524288 | tf_op jit(solution)/shard_map/all_to_all | solution.py:447
  111.5 0.6 norm.1
  112.2 8.7 %all-to-all-done.2 = bf16[8,64,256]{2,1,0:T(8,128)(2,1)S(1)} async-done(((bf16[8,64,256]{2,1,0:T(8,128)(2,1)}), bf16[8,64,256]{2,1,0:T(8,128)(2,1)S(1)}, u32[]{:S(2)}, u32[]{:S(2)}) %all-to-all-start.2) | async-done | bytes 262176 | tf_op jit(solution)/shard_map/all_to_all | solution.py:447
  120.9 7.7 %all-to-all-start.6 = ((f32[64,1,128]{2,1,0:T(1,128)}), f32[64,1,128]{2,1,0:T(1,128)S(1)}, u32[]{:S(2)}, u32[]{:S(2)}) async-start(f32[64,1,128]{2,1,0:T(1,128)} %get-tuple-element.20), calls=%async_computation.6 | async-start | bytes 65536 | tf_op jit(solution)/shard_map/all_to_all | solution.py:463
  128.6 0.7 convert_reduce_fusion
  129.2 8.4 %all-to-all-done.6.pairs = f32[64,1,128]{2,1,0:T(1,128)S(1)} async-done(((f32[64,1,128]{2,1,0:T(1,128)}), f32[64,1,128]{2,1,0:T(1,128)S(1)}, u32[]{:S(2)}, u32[]{:S(2)}) %all-to-all-start.6) | async-done | bytes 32800 | tf_op jit(solution)/shard_map/all_to_all | solution.py:463
  137.6 0.7 clip.1
  (17 shorter events, 0.0 us)
Async XLA Ops:
  0.6 1.0 copy-start.2
  1.6 1.2 copy-start.5
  2.8 0.8 copy-start.11
  3.6 0.7 copy-start.12
  4.2 0.7 copy-start.13
  28.1 19.7 %all-to-all-start.1 = ((bf16[32,32,128]{2,1,0:T(8,128)(2,1)}), bf16[32,32,128]{2,1,0:T(8,128)(2,1)S(1)}, u32[]{:S(2)}, u32[]{:S(2)}) async-start(bf16[32,32,128]{2,1,0:T(8,128)(2,1)} %scan.1), calls=%async_computation.1 | async-start | bytes 524288 | tf_op jit(solution)/shard_map/all_to_all | solution.py:397
  35.3 12.5 %copy-start.3 = (bf16[1,512,256]{2,1,0:T(8,128)(2,1)S(1)}, bf16[1,512,256]{2,1,0:T(8,128)(2,1)}, u32[]{:S(2)}) copy-start(bf16[1,512,256]{2,1,0:T(8,128)(2,1)} %param.10) | copy-start | bytes 786436
  35.3 34.9 %copy-start.6 = (bf16[1,512,1024]{2,1,0:T(8,128)(2,1)S(1)}, bf16[1,512,1024]{2,1,0:T(8,128)(2,1)}, u32[]{:S(2)}) copy-start(bf16[1,512,1024]{2,1,0:T(8,128)(2,1)} %param.14) | copy-start | bytes 3145732
  47.8 1.2 copy-start
  49.0 0.9 copy-start.7
  50.0 1.0 copy-start.10
  51.0 50.3 %copy-start.1 = (bf16[512,1024]{1,0:T(8,128)(2,1)S(1)}, bf16[512,1024]{1,0:T(8,128)(2,1)}, u32[]{:S(2)}) copy-start(bf16[512,1024]{1,0:T(8,128)(2,1)} %get-tuple-element.13.xl) | copy-start | bytes 3145732
  51.0 50.3 %copy-start.8 = (f32[5,16,512]{2,1,0:T(8,128)S(1)}, f32[5,16,512]{2,1,0:T(8,128)}, u32[]{:S(2)}) copy-start(f32[5,16,512]{2,1,0:T(8,128)} %get-tuple-element.15.vec) | copy-start | bytes 491524
  51.0 50.3 %copy-start.9 = (f32[512,256]{1,0:T(8,128)S(1)}, f32[512,256]{1,0:T(8,128)}, u32[]{:S(2)}) copy-start(f32[512,256]{1,0:T(8,128)} %get-tuple-element.16.gm) | copy-start | bytes 1572868
  98.0 10.1 %all-to-all-start.5 = ((f32[8,8,128]{2,1,0:T(8,128)}), f32[8,8,128]{2,1,0:T(8,128)S(1)}, u32[]{:S(2)}, u32[]{:S(2)}) async-start(f32[8,8,128]{2,1,0:T(8,128)} %get-tuple-element.19), calls=%async_computation.5 | async-start | bytes 65536 | tf_op jit(solution)/shard_map/all_to_all | solution.py:456
  101.3 1.6 %copy-start.4 = (f32[512,1024]{1,0:T(8,128)S(1)}, f32[512,1024]{1,0:T(8,128)}, u32[]{:S(2)}) copy-start(f32[512,1024]{1,0:T(8,128)} %get-tuple-element.14.rdt) | copy-start | bytes 6291460
  108.1 12.8 %all-to-all-start.2 = ((bf16[8,64,256]{2,1,0:T(8,128)(2,1)}), bf16[8,64,256]{2,1,0:T(8,128)(2,1)S(1)}, u32[]{:S(2)}, u32[]{:S(2)}) async-start(bf16[8,64,256]{2,1,0:T(8,128)(2,1)} %get-tuple-element.18), calls=%async_computation.2 | async-start | bytes 524288 | tf_op jit(solution)/shard_map/all_to_all | solution.py:447
  120.9 16.8 %all-to-all-start.6 = ((f32[64,1,128]{2,1,0:T(1,128)}), f32[64,1,128]{2,1,0:T(1,128)S(1)}, u32[]{:S(2)}, u32[]{:S(2)}) async-start(f32[64,1,128]{2,1,0:T(1,128)} %get-tuple-element.20), calls=%async_computation.6 | async-start | bytes 65536 | tf_op jit(solution)/shard_map/all_to_all | solution.py:463
